TPU v7x, 512 devices: a whole 4x8x8 slice. The times are simulated.
512 devices in a mesh: stream: 8 (over y), span: 16 (over z, core), vert: 4 (over x).
Axes of the slice: x: 4, y: 8, z: 8, core: 2. Of those that a mesh axis runs over, the one named last changes fastest.
Arguments:
- fields: float32 [5, 128, 256, 1024], P(None, 'vert', 'span', 'stream'), may hold values from -6 to 6
- solid_frac: float32 [128, 256, 1024], P('vert', 'span', 'stream'), may hold values from 0 to 1
- panels: float32 [32768, 5, 256], P(('stream', 'span', 'vert')), may hold values from -0.015625 to 0.015625
- panel_owner: int32 [32768, 1], P(('stream', 'span', 'vert')), may hold values from 0 to 63; in each aligned block of 64 rows (0 to 63, 64 to 127, ...) at most 2 rows name the same one
- deck_cells: int32 [4, 16, 8, 2048], P('vert', 'span', 'stream'), may hold values from 0 to 65535
- deck_geom: float32 [4, 16, 8, 3, 2048], P('vert', None, 'stream'), may hold values from -6 to 6
- strip_ids: int32 [4, 16, 8, 2048], P('vert', None, 'stream'), may hold values from 0 to 63, as said below
- mode_shapes: float32 [3, 64, 32], replicated, may hold values from -0.0034179688 to 0.0034179688
Outputs:
- new_fields: float32 [5, 128, 256, 1024], P(None, 'vert', 'span', 'stream')
- modal_force: float32 [32], replicated
Inputs may be any that keep to these rules, and one draw needn't show every extreme that they name: `panel_owner`: tile number s * 4 + v for along-deck tile s and vertical tile v. Among the 64 panels of one device no tile is named more than 2 times; some device names some tile exactly 2 times. `strip_ids`: cells of along-deck tile s belong to strips s * 4 to (s + 1) * 4 - 1.
All inputs are finite; a program needn't handle non-finite values.
Results may differ from a plain program's by a relative error of at most 0.00012.
Values sent between devices are 32-bit elements; how exact they have to be, the bound alone decides.
No kernel may reach another device: no remote copies, remote signals or barrier semaphores. Data moves between devices by JAX's collectives and lax.ppermute only.
A program may use at most 128 MiB of HBM per device.

v0:
```python
import math
import jax
import jax.numpy as jnp
from jax import lax
from jax.sharding import PartitionSpec as P

CAP = 2
time_step = 0.15
viscous = 0.05
heat_diff = 0.03
sound_sq = 1.0
buoyant = 0.5
penalty = 0.5
relax_time = 0.5
relax_depth = 8.0
wave_cols = 16


def extended(block, sides, width):
    for axis, dim in sides:
        count = lax.axis_size(axis)
        forward = [(i, i + 1) for i in range(count - 1)]
        backward = [(target, source) for source, target in forward]
        low = lax.ppermute(
            lax.slice_in_dim(block, block.shape[dim] - width, None, axis=dim), axis, forward
        )
        high = lax.ppermute(lax.slice_in_dim(block, 0, width, axis=dim), axis, backward)
        block = jnp.concatenate([low, block, high], axis=dim)
    return block


def wave_basis(heights, widths, total_z, total_y, spec):
    modes = jnp.arange(spec, dtype=jnp.int32)
    across = (modes % wave_cols)[:, None, None]
    upward = (modes // wave_cols)[:, None, None]
    period = total_y * total_z
    phase = (
        across * widths[None, None, :] * total_z + upward * heights[None, :, None] * total_y
    ) % period
    angle = phase.astype(jnp.float32) * (2.0 * math.pi / period)
    return jnp.concatenate([jnp.cos(angle), jnp.sin(angle)], axis=0)


def relax_weights(positions, limit):
    spots = positions.astype(jnp.float32)
    return jnp.where(positions < limit, jnp.exp(-spots / relax_depth) / relax_time, 0.0)


def rates(padded, solid_frac, relax_rate, target_plane):
    centre = padded[:, 1:-1, 1:-1, 1:-1]
    east_side = padded[:, 1:-1, 1:-1, 2:]
    west_side = padded[:, 1:-1, 1:-1, :-2]
    north_side = padded[:, 1:-1, 2:, 1:-1]
    south_side = padded[:, 1:-1, :-2, 1:-1]
    upper_side = padded[:, 2:, 1:-1, 1:-1]
    lower_side = padded[:, :-2, 1:-1, 1:-1]
    grad_x = 0.5 * (east_side - west_side)
    grad_y = 0.5 * (north_side - south_side)
    grad_z = 0.5 * (upper_side - lower_side)
    laplace = (
        east_side + west_side + north_side + south_side + upper_side + lower_side - 6.0 * centre
    )
    speed_x = centre[0]
    speed_y = centre[1]
    speed_z = centre[2]
    carried = speed_x * grad_x + speed_y * grad_y + speed_z * grad_z
    coeffs = jnp.array([viscous, viscous, viscous, viscous, heat_diff], jnp.float32)[
        :, None, None, None
    ]
    damping = solid_frac / penalty
    nudging = relax_rate[None, None, None, :] * (target_plane[:, :, :, None] - centre)
    common = coeffs * laplace - carried + nudging
    extra_terms = jnp.stack(
        [
            -grad_x[3] - damping * speed_x,
            -grad_y[3] - damping * speed_y,
            -grad_z[3] - damping * speed_z + buoyant * centre[4],
            -sound_sq * (grad_x[0] + grad_y[1] + grad_z[2]),
            jnp.zeros_like(speed_x),
        ]
    )
    return common + extra_terms


def pack_slots(flat_panels, target_tile, chosen, tile_count):
    running = jnp.cumsum(chosen, axis=0) - 1
    slot_rank = jnp.sum(chosen * running, axis=1)
    slot_index = target_tile * CAP + slot_rank
    dispatch = (
        slot_index[None, :] == jnp.arange(tile_count * CAP, dtype=jnp.int32)[:, None]
    ).astype(jnp.float32)
    return jnp.dot(dispatch, flat_panels, precision=lax.Precision.HIGHEST)


def strip_forces(traction, labels, strip_count):
    columns = jnp.arange(strip_count, dtype=jnp.int32)

    def add_row(running, item_pair):
        row_values, row_labels = item_pair
        member = (row_labels[:, None] == columns[None, :]).astype(jnp.float32)
        return (running + jnp.dot(row_values, member, precision=lax.Precision.HIGHEST), None)

    start_value = jnp.zeros((traction.shape[1], strip_count), jnp.float32)
    summed, ignored = lax.scan(add_row, start_value, (traction, labels))
    return summed


def on_device(
    fields, solid_frac, panels, panel_owner, deck_cells, deck_geom, strip_ids, mode_shapes
):
    depth_cells = fields.shape[1]
    span_cells = fields.shape[2]
    wind_cells = fields.shape[3]
    n_span = lax.axis_size("span")
    n_vert = lax.axis_size("vert")
    stream_pos = lax.axis_index("stream")
    span_pos = lax.axis_index("span")
    vert_pos = lax.axis_index("vert")
    tile_count = n_span * n_vert
    held_panels = panels.shape[0]
    spec_cols = panels.shape[2]
    flat_panels = panels.reshape(held_panels, 5 * spec_cols)
    target_tile = panel_owner[:, 0]
    chosen = (target_tile[:, None] == jnp.arange(tile_count, dtype=jnp.int32)[None, :]).astype(
        jnp.int32
    )
    outgoing = pack_slots(flat_panels, target_tile, chosen, tile_count)
    arrived = lax.all_to_all(
        outgoing.reshape(tile_count, CAP * 5 * spec_cols),
        ("span", "vert"),
        split_axis=0,
        concat_axis=0,
        tiled=True,
    )
    coeffs = jnp.sum(arrived.reshape(-1, 5 * spec_cols), axis=0)
    coeffs = coeffs.reshape(5, spec_cols)
    heights = vert_pos * depth_cells + jnp.arange(depth_cells, dtype=jnp.int32)
    widths = span_pos * span_cells + jnp.arange(span_cells, dtype=jnp.int32)
    wave_table = wave_basis(
        heights, widths, depth_cells * n_vert, span_cells * n_span, spec_cols // 2
    )
    wave_table = wave_table.reshape(spec_cols, depth_cells * span_cells)
    partial_value = jnp.dot(coeffs, wave_table, precision=lax.Precision.HIGHEST)
    inflow_plane = lax.psum(partial_value, "stream").reshape(5, depth_cells, span_cells)
    target_plane = inflow_plane + jnp.array([1.0, 0.0, 0.0, 0.0, 0.0], jnp.float32)[:, None, None]
    wind_first = stream_pos * wind_cells
    relax_rate = relax_weights(
        wind_first + jnp.arange(wind_cells, dtype=jnp.int32), wind_cells // 2
    )

    def advance(state):
        padded = extended(state, (("stream", 3), ("span", 2), ("vert", 1)), 1)
        return rates(padded, solid_frac, relax_rate, target_plane)

    first_update = fields + time_step * advance(fields)
    second_rate = advance(first_update)
    new_fields = 0.5 * (fields + first_update + time_step * second_rate)
    pressure = new_fields[3].reshape(-1)
    sampled = pressure[deck_cells[0, 0, 0]]
    strip_count = mode_shapes.shape[1]
    rows_all = lax.all_gather(sampled.reshape(1, 1, 1, -1), "span", axis=1, tiled=True)
    traction = rows_all[0, :, 0][:, None, :] * deck_geom[0, :, 0]
    forces = strip_forces(traction, strip_ids[0, :, 0], strip_count)
    modal_part = jnp.einsum("cj,cjm->m", forces, mode_shapes, precision=lax.Precision.HIGHEST)
    modal_force = lax.psum(modal_part, ("stream", "vert"))
    return (new_fields, modal_force)


def solution(mesh):
    return jax.shard_map(
        on_device,
        mesh=mesh,
        in_specs=(
            P(None, "vert", "span", "stream"),
            P("vert", "span", "stream"),
            P(("stream", "span", "vert"), None, None),
            P(("stream", "span", "vert"), None),
            P("vert", "span", "stream", None),
            P("vert", None, "stream", None, None),
            P("vert", None, "stream", None),
            P(),
        ),
        out_specs=(P(None, "vert", "span", "stream"), P()),
        check_vma=False,
    )
```

profile of v0, /device:TPU:64, one launch (start us, length us, event | category | flops | bytes accessed | tf_op | source)
XLA Modules:
  0.0 263.3 jit_solution(5278629360200519969)
XLA Ops:
  0.6 2.2 fusion.52
  5.3 4.5 %collective-permute-start.1 = (f32[5,32,16,1]{1,2,3,0:T(8,128)S(1)}, f32[5,32,16,1]{1,2,3,0:T(8,128)S(1)}, u32[]{:S(2)}, u32[]{:S(2)}) collective-permute-start(f32[5,32,16,1]{1,2,3,0:T(8,128)S(1)} %copy.56), channel_id=1, source_target_pairs={{0,64},{64,128},{128,192},{192,256},{256,320},{320,384},{384,448},... | collective-permute-start | bytes 30728 | tf_op jit(solution)/shard_map/ppermute | solution.py:24
  12.2 13.3 %all-to-all-start = ((f32[64,1,2560]{2,1,0:T(1,128)}), f32[64,1,2560]{2,1,0:T(1,128)}, u32[]{:S(2)}, u32[]{:S(2)}) async-start(f32[64,1,2560]{2,1,0:T(1,128)} %all_to_all.8), calls=%async_computation | async-start | bytes 1310720 | tf_op jit(solution)/shard_map/all_to_all | solution.py:128
  30.7 2.5 pad_maximum_fusion.39
  33.2 2.0 collective-permute-start.2
  35.2 2.3 collective-permute-start.3
  37.5 4.0 %collective-permute-done.2 = f32[5,32,1,130]{3,2,1,0:T(1,128)S(1)} collective-permute-done((f32[5,32,1,130]{3,2,1,0:T(1,128)S(1)}, f32[5,32,1,130]{3,2,1,0:T(1,128)S(1)}, u32[]{:S(2)}, u32[]{:S(2)}) %collective-permute-start.2) | collective-permute-done | bytes 83232 | tf_op jit(solution)/shard_map/ppermute | solution.py:27
  44.5 4.7 %collective-permute-start.5 = (f32[5,1,18,130]{3,2,1,0:T(8,128)S(1)}, f32[5,1,18,130]{3,2,1,0:T(8,128)S(1)}, u32[]{:S(2)}, u32[]{:S(2)}) collective-permute-start(f32[5,1,18,130]{3,2,1,0:T(8,128)S(1)} %get-tuple-element.71), channel_id=1, source_target_pairs={{0,1},{1,2},{2,3},{4,5},{5,6},{6,7},{8,9},{9,10},{10,11},{12,13},{... | collective-permute-start | bytes 140408 | tf_op jit(solution)/shard_map/ppermute | solution.py:24
  51.7 3.2 %broadcast_multiply_fusion.3 = (f32[5,32,16,128]{3,2,1,0:T(8,128)S(1)}, f32[5,32,16,128]{3,2,1,0:T(8,128)S(1)}) fusion(f32[5,1,18,130]{3,2,1,0:T(8,128)S(1)} %collective-permute-done.4, f32[5,32,1,130]{3,2,1,0:T(1,128)S(1)} %collective-permute-done.2, f32[5,32,16,1]{3,2,1,0:T(8,128)S(1)} %copy.37, f32[5,32,16,128]{3,2,1,0:T(8,128)S(1)} %copy-done.1, ...), kind=kLoop, calls=%fused_computation.50 | loop fusion | flops 5242880 | bytes 4212640 | tf_op jit(solution)/shard_map/mul | solution.py:59
  58.7 2.6 %reduce = f32[64,2560]{1,0:T(8,128)S(1)} reduce(f32[64,1,2560]{2,1,0:T(1,128)} %all-to-all-done, f32[]{:T(128)} %constant.123), dimensions={1}, to_apply=%all_to_all.7.reduce_sub_computation | reduce | bytes 1310724 | tf_op jit(solution)/shard_map/all_to_all | solution.py:128
  63.1 30.8 %psum.14 = f32[5,32,16]{2,1,0:T(8,128)S(1)} all-reduce(f32[5,32,16]{2,1,0:T(8,128)S(1)} %reshape.200), channel_id=1, replica_groups=mesh['stream'=8,'span'=16,'vert'=4] {'stream'}, use_global_device_ids=true, to_apply=%region_3.4 | all-reduce | flops 2560 | bytes 20480 | tf_op jit(solution)/shard_map/psum | solution.py:144
  94.0 7.5 %multiply_add_fusion = f32[5,32,16,128]{3,2,1,0:T(8,128)S(1)} fusion(f32[5,32,16,128]{3,2,1,0:T(8,128)S(1)} %copy-done.1, f32[5,32,16,128]{3,2,1,0:T(8,128)} %broadcast_dynamic-update-slice_fusion.1, f32[5,32,16]{2,1,0:T(8,128)S(1)} %broadcast_add_fusion.1, f32[128]{0:T(128)S(1)} %compare_select_fusion.1, f32[32,16,128]{2,1,0:T(8,128)} %get-tuple-element.87, ...), kind=kLoop, calls=%fused_computation.45 | loop fusion | flops 13434880 | bytes 5009844 | tf_op jit(solution)/shard_map/add | solution.py:155
  108.5 4.5 %collective-permute-start.7 = (f32[5,32,16,1]{1,2,3,0:T(8,128)S(1)}, f32[5,32,16,1]{1,2,3,0:T(8,128)S(1)}, u32[]{:S(2)}, u32[]{:S(2)}) collective-permute-start(f32[5,32,16,1]{1,2,3,0:T(8,128)S(1)} %copy.46), channel_id=1, source_target_pairs={{0,64},{64,128},{128,192},{192,256},{256,320},{320,384},{384,448},... | collective-permute-start | bytes 30728 | tf_op jit(solution)/shard_map/ppermute | solution.py:24
  116.4 2.9 %pad_maximum_fusion.36 = (f32[5,32,1,130]{3,2,1,0:T(1,128)S(1)}, f32[5,32,1,130]{3,2,1,0:T(1,128)S(1)}) fusion(f32[5,32,16,1]{3,2,1,0:T(8,128)} %copy.45, f32[5,32,16,128]{3,2,1,0:T(8,128)S(1)} %multiply_add_fusion, f32[5,32,16,1]{3,2,1,0:T(8,128)} %copy.47), kind=kLoop, calls=%fused_computation.118 | loop fusion | flops 83200 | bytes 1497600 | tf_op jit(solution)/shard_map/concatenate | solution.py:28
  119.3 2.1 collective-permute-start.8
  121.4 2.6 collective-permute-start.9
  124.2 3.8 %collective-permute-done.9 = f32[5,32,1,130]{3,2,1,0:T(1,128)S(1)} collective-permute-done((f32[5,32,1,130]{3,2,1,0:T(1,128)S(1)}, f32[5,32,1,130]{3,2,1,0:T(1,128)S(1)}, u32[]{:S(2)}, u32[]{:S(2)}) %collective-permute-start.9) | collective-permute-done | bytes 83232 | tf_op jit(solution)/shard_map/ppermute | solution.py:24
  129.5 5.0 %collective-permute-start.11 = (f32[5,1,18,130]{3,2,1,0:T(8,128)S(1)}, f32[5,1,18,130]{3,2,1,0:T(8,128)S(1)}, u32[]{:S(2)}, u32[]{:S(2)}) collective-permute-start(f32[5,1,18,130]{3,2,1,0:T(8,128)S(1)} %get-tuple-element.69), channel_id=1, source_target_pairs={{0,1},{1,2},{2,3},{4,5},{5,6},{6,7},{8,9},{9,10},{10,11},{12,13},{... | collective-permute-start | bytes 140408 | tf_op jit(solution)/shard_map/ppermute | solution.py:24
  136.9 3.1 %broadcast_multiply_fusion = (f32[5,32,16,128]{3,2,1,0:T(8,128)S(1)}, f32[5,32,16,128]{3,2,1,0:T(8,128)S(1)}) fusion(f32[5,1,18,130]{3,2,1,0:T(8,128)S(1)} %collective-permute-done.10, f32[5,32,1,130]{3,2,1,0:T(1,128)S(1)} %collective-permute-done.8, f32[5,32,16,1]{3,2,1,0:T(8,128)S(1)} %copy-done.4, f32[5,32,16,128]{3,2,1,0:T(8,128)S(1)} %multiply_add_fusion, ...), kind=kLoop, calls=%fused_computation.47 | loop fusion | flops 5242880 | bytes 4212640 | tf_op jit(solution)/shard_map/mul | solution.py:59
  140.4 5.0 %add_multiply_fusion = f32[5,32,16,128]{3,2,1,0:T(8,128)S(1)} fusion(f32[5,32,16,128]{3,2,1,0:T(8,128)S(1)} %broadcast_dynamic-update-slice_fusion, f32[5,32,16,128]{3,2,1,0:T(8,128)S(1)} %multiply_add_fusion, f32[5,32,16,128]{3,2,1,0:T(8,128)S(1)} %copy-done.1, f32[32,16,128]{2,1,0:T(8,128)S(1)} %get-tuple-element.82, ...), kind=kLoop, calls=%fused_computation.44 | loop fusion | flops 14090240 | bytes 6320564 | tf_op jit(solution)/shard_map/mul | solution.py:157
  146.5 11.8 %gather_fusion = f32[2048]{0:T(1024)S(1)} fusion(f32[65536]{0:T(1024)S(1)} %bitcast.150, s32[2048]{0:T(1024)S(1)} %broadcast_clamp_fusion), kind=kCustom, calls=%fused_computation | custom fusion | bytes 24576 | tf_op jit(solution)/shard_map/gather | solution.py:159
  158.2 16.8 %all-gather = f32[32768]{0:T(1024)S(1)} all-gather(f32[2048]{0:T(1024)S(1)} %gather_fusion), channel_id=2, replica_groups=mesh['stream'=8,'span'=16,'vert'=4] {'span'}, dimensions={0}, use_global_device_ids=true | all-gather | bytes 139264 | tf_op jit(solution)/shard_map/all_gather | solution.py:161
  175.2 10.6 %while.11 = (s32[]{:T(128)}, f32[3,64]{1,0:T(4,128)S(1)}, f32[16,3,2048]{2,0,1:T(8,128)S(1)}, s32[16,2048]{1,0:T(8,128)S(1)}, s32[]{:T(128)}, /*index=5*/s32[]{:T(128)}) while((s32[]{:T(128)}, f32[3,64]{1,0:T(4,128)S(1)}, f32[16,3,2048]{2,0,1:T(8,128)S(1)}, s32[16,2048]{1,0:T(8,128)S(1)}, s32[]{:T(128)}, /*index=5*/s32[]{:T(128)}) %tuple.46), condition=%wide.region_5.6_spmd.clone, body=%wide.region_4.5_spmd.clone.sunk | while | flops 4850051 | bytes 99927 | solution.py:104
  186.0 77.3 %psum.15 = f32[32]{0:T(128)} all-reduce(f32[32]{0:T(128)S(1)} %convolution_bitcast_fusion), channel_id=1, replica_groups=mesh['stream'=8,'span'=16,'vert'=4] {'stream','vert'}, use_global_device_ids=true, to_apply=%region_6.7 | all-reduce | flops 32 | bytes 256 | tf_op jit(solution)/shard_map/psum | solution.py:165
  (152 shorter events, 46.9 us)
Async XLA Ops:
  0.6 185.2 %copy-start = (f32[3,64,32]{1,2,0:T(8,128)S(1)}, f32[3,64,32]{1,2,0:T(8,128)}, u32[]{:S(2)}) copy-start(f32[3,64,32]{1,2,0:T(8,128)} %param.20) | copy-start | bytes 73732
  3.4 25.0 %collective-permute-start = (f32[5,32,16,1]{1,2,3,0:T(8,128)S(1)}, f32[5,32,16,1]{1,2,3,0:T(8,128)S(1)}, u32[]{:S(2)}, u32[]{:S(2)}) collective-permute-start(f32[5,32,16,1]{1,2,3,0:T(8,128)S(1)} %copy.55), channel_id=1, source_target_pairs={{64,0},{128,64},{192,128},{256,192},{320,256},{384,320},{448,384},... | collective-permute-start | bytes 30728 | tf_op jit(solution)/shard_map/ppermute | solution.py:27
  5.3 23.7 %collective-permute-start.1 = (f32[5,32,16,1]{1,2,3,0:T(8,128)S(1)}, f32[5,32,16,1]{1,2,3,0:T(8,128)S(1)}, u32[]{:S(2)}, u32[]{:S(2)}) collective-permute-start(f32[5,32,16,1]{1,2,3,0:T(8,128)S(1)} %copy.56), channel_id=1, source_target_pairs={{0,64},{64,128},{128,192},{192,256},{256,320},{320,384},{384,448},... | collective-permute-start | bytes 30728 | tf_op jit(solution)/shard_map/ppermute | solution.py:24
  10.7 14.8 %copy-start.1 = (f32[5,32,16,128]{3,2,1,0:T(8,128)S(1)}, f32[5,32,16,128]{3,2,1,0:T(8,128)}, u32[]{:S(2)}) copy-start(f32[5,32,16,128]{3,2,1,0:T(8,128)} %param.13) | copy-start | bytes 3932164
  12.2 14.2 %copy-start.13 = (s32[1,1,1,2048]{3,2,1,0:T(1,128)S(1)}, s32[1,1,1,2048]{3,2,1,0:T(1,128)}, u32[]{:S(2)}) copy-start(s32[1,1,1,2048]{3,2,1,0:T(1,128)} %param.17) | copy-start | bytes 24580
  12.2 46.5 %all-to-all-start = ((f32[64,1,2560]{2,1,0:T(1,128)}), f32[64,1,2560]{2,1,0:T(1,128)}, u32[]{:S(2)}, u32[]{:S(2)}) async-start(f32[64,1,2560]{2,1,0:T(1,128)} %all_to_all.8), calls=%async_computation | async-start | bytes 1310720 | tf_op jit(solution)/shard_map/all_to_all | solution.py:128
  29.1 22.7 %copy-start.2 = (f32[5,32,16,1]{3,2,1,0:T(8,128)}, f32[5,32,16,1]{3,2,1,0:T(8,128)S(1)}, u32[]{:S(2)}) copy-start(f32[5,32,16,1]{3,2,1,0:T(8,128)S(1)} %copy.37) | copy-start | bytes 30724
  30.7 12.4 %copy-start.3 = (f32[5,32,16,1]{3,2,1,0:T(8,128)S(1)}, f32[5,32,16,1]{3,2,1,0:T(8,128)}, u32[]{:S(2)}) copy-start(f32[5,32,16,1]{3,2,1,0:T(8,128)} %copy.39) | copy-start | bytes 30724
  33.2 8.4 %collective-permute-start.2 = (f32[5,32,1,130]{3,2,1,0:T(1,128)S(1)}, f32[5,32,1,130]{3,2,1,0:T(1,128)S(1)}, u32[]{:S(2)}, u32[]{:S(2)}) collective-permute-start(f32[5,32,1,130]{3,2,1,0:T(1,128)S(1)} %get-tuple-element.80), channel_id=1, source_target_pairs={{4,0},{8,4},{12,8},{16,12},{20,16},{24,20},{28,24},{32,28},{36,32}... | collective-permute-start | bytes 249608 | tf_op jit(solution)/shard_map/ppermute | solution.py:27
  35.2 7.9 %collective-permute-start.3 = (f32[5,32,1,130]{3,2,1,0:T(1,128)S(1)}, f32[5,32,1,130]{3,2,1,0:T(1,128)S(1)}, u32[]{:S(2)}, u32[]{:S(2)}) collective-permute-start(f32[5,32,1,130]{3,2,1,0:T(1,128)S(1)} %get-tuple-element.79), channel_id=1, source_target_pairs={{0,4},{4,8},{8,12},{12,16},{16,20},{20,24},{24,28},{28,32},{32,36}... | collective-permute-start | bytes 249608 | tf_op jit(solution)/shard_map/ppermute | solution.py:24
  43.2 7.3 %collective-permute-start.4 = (f32[5,1,18,130]{3,2,1,0:T(8,128)S(1)}, f32[5,1,18,130]{3,2,1,0:T(8,128)S(1)}, u32[]{:S(2)}, u32[]{:S(2)}) collective-permute-start(f32[5,1,18,130]{3,2,1,0:T(8,128)S(1)} %get-tuple-element.72), channel_id=1, source_target_pairs={{1,0},{2,1},{3,2},{5,4},{6,5},{7,6},{9,8},{10,9},{11,10},{13,12},{... | collective-permute-start | bytes 140408 | tf_op jit(solution)/shard_map/ppermute | solution.py:27
  44.5 7.2 %collective-permute-start.5 = (f32[5,1,18,130]{3,2,1,0:T(8,128)S(1)}, f32[5,1,18,130]{3,2,1,0:T(8,128)S(1)}, u32[]{:S(2)}, u32[]{:S(2)}) collective-permute-start(f32[5,1,18,130]{3,2,1,0:T(8,128)S(1)} %get-tuple-element.71), channel_id=1, source_target_pairs={{0,1},{1,2},{2,3},{4,5},{5,6},{6,7},{8,9},{9,10},{10,11},{12,13},{... | collective-permute-start | bytes 140408 | tf_op jit(solution)/shard_map/ppermute | solution.py:24
  61.3 32.6 %copy-start.16 = (f32[5]{0:T(128)S(1)}, f32[5]{0:T(128)}, u32[]{:S(2)}) copy-start(f32[5]{0:T(128)} %constant.116.clone) | copy-start | bytes 64
  61.4 32.6 %copy-start.15 = (f32[5]{0:T(128)S(1)}, f32[5]{0:T(128)}, u32[]{:S(2)}) copy-start(f32[5]{0:T(128)} %constant.117.clone) | copy-start | bytes 64
  103.5 9.7 %copy-start.12 = (s32[1,16,1,2048]{3,2,1,0:T(1,128)S(1)}, s32[1,16,1,2048]{3,2,1,0:T(1,128)}, u32[]{:S(2)}) copy-start(s32[1,16,1,2048]{3,2,1,0:T(1,128)} %param.19) | copy-start | bytes 393220
  105.4 7.8 %collective-permute-start.6 = (f32[5,32,16,1]{1,2,3,0:T(8,128)S(1)}, f32[5,32,16,1]{1,2,3,0:T(8,128)S(1)}, u32[]{:S(2)}, u32[]{:S(2)}) collective-permute-start(f32[5,32,16,1]{1,2,3,0:T(8,128)S(1)} %copy.44), channel_id=1, source_target_pairs={{64,0},{128,64},{192,128},{256,192},{320,256},{384,320},{448,384},... | collective-permute-start | bytes 30728 | tf_op jit(solution)/shard_map/ppermute | solution.py:27
  108.5 6.3 %collective-permute-start.7 = (f32[5,32,16,1]{1,2,3,0:T(8,128)S(1)}, f32[5,32,16,1]{1,2,3,0:T(8,128)S(1)}, u32[]{:S(2)}, u32[]{:S(2)}) collective-permute-start(f32[5,32,16,1]{1,2,3,0:T(8,128)S(1)} %copy.46), channel_id=1, source_target_pairs={{0,64},{64,128},{128,192},{192,256},{256,320},{320,384},{384,448},... | collective-permute-start | bytes 30728 | tf_op jit(solution)/shard_map/ppermute | solution.py:24
  116.4 11.6 %copy-start.5 = (f32[5,32,16,1]{3,2,1,0:T(8,128)S(1)}, f32[5,32,16,1]{3,2,1,0:T(8,128)}, u32[]{:S(2)}) copy-start(f32[5,32,16,1]{3,2,1,0:T(8,128)} %copy.47) | copy-start | bytes 30724
  119.3 8.7 %copy-start.4 = (f32[5,32,16,1]{3,2,1,0:T(8,128)S(1)}, f32[5,32,16,1]{3,2,1,0:T(8,128)}, u32[]{:S(2)}) copy-start(f32[5,32,16,1]{3,2,1,0:T(8,128)} %copy.45) | copy-start | bytes 30724
  119.3 4.9 %collective-permute-start.8 = (f32[5,32,1,130]{3,2,1,0:T(1,128)S(1)}, f32[5,32,1,130]{3,2,1,0:T(1,128)S(1)}, u32[]{:S(2)}, u32[]{:S(2)}) collective-permute-start(f32[5,32,1,130]{3,2,1,0:T(1,128)S(1)} %get-tuple-element.76), channel_id=1, source_target_pairs={{4,0},{8,4},{12,8},{16,12},{20,16},{24,20},{28,24},{32,28},{36,32}... | collective-permute-start | bytes 249608 | tf_op jit(solution)/shard_map/ppermute | solution.py:27
  121.4 6.6 %collective-permute-start.9 = (f32[5,32,1,130]{3,2,1,0:T(1,128)S(1)}, f32[5,32,1,130]{3,2,1,0:T(1,128)S(1)}, u32[]{:S(2)}, u32[]{:S(2)}) collective-permute-start(f32[5,32,1,130]{3,2,1,0:T(1,128)S(1)} %get-tuple-element.75), channel_id=1, source_target_pairs={{0,4},{4,8},{8,12},{12,16},{16,20},{20,24},{24,28},{28,32},{32,36}... | collective-permute-start | bytes 249608 | tf_op jit(solution)/shard_map/ppermute | solution.py:24
  128.2 7.4 %collective-permute-start.10 = (f32[5,1,18,130]{3,2,1,0:T(8,128)S(1)}, f32[5,1,18,130]{3,2,1,0:T(8,128)S(1)}, u32[]{:S(2)}, u32[]{:S(2)}) collective-permute-start(f32[5,1,18,130]{3,2,1,0:T(8,128)S(1)} %get-tuple-element.70), channel_id=1, source_target_pairs={{1,0},{2,1},{3,2},{5,4},{6,5},{7,6},{9,8},{10,9},{11,10},{13,12},{... | collective-permute-start | bytes 140408 | tf_op jit(solution)/shard_map/ppermute | solution.py:27
  129.5 7.4 %collective-permute-start.11 = (f32[5,1,18,130]{3,2,1,0:T(8,128)S(1)}, f32[5,1,18,130]{3,2,1,0:T(8,128)S(1)}, u32[]{:S(2)}, u32[]{:S(2)}) collective-permute-start(f32[5,1,18,130]{3,2,1,0:T(8,128)S(1)} %get-tuple-element.69), channel_id=1, source_target_pairs={{0,1},{1,2},{2,3},{4,5},{5,6},{6,7},{8,9},{9,10},{10,11},{12,13},{... | collective-permute-start | bytes 140408 | tf_op jit(solution)/shard_map/ppermute | solution.py:24
  146.4 28.6 %copy-start.10 = (f32[1,16,1,3,2048]{4,2,3,1,0:T(1,128)S(1)}, f32[1,16,1,3,2048]{4,2,3,1,0:T(1,128)}, u32[]{:S(2)}) copy-start(f32[1,16,1,3,2048]{4,2,3,1,0:T(1,128)} %param.18) | copy-start | bytes 1179652
  (6 other events, 27.6 us)
where the time goes:
time: 264 us; the launch traced here: 263 us
  blocking collectives  125 us (47%)
  starting transfers between devices  46.3 us (18%)
  other arithmetic  36.1 us (14%)
  local copies, waits for them, and re-layouts  30.7 us (12%)
  waiting for transfers between devices  12.1 us (5%)
  matrix products  11.3 us (4%)
    psum x1, blocking collectives, on_device(): modal_force = lax.psum(modal_part, ('stream', 'vert'))  77.3 us
    psum x1, blocking collectives, on_device(): lax.psum(partial_value, 'stream').reshape(5, depth_cells, span_cells)  30.8 us
    ppermute x6, starting transfers between devices, extended(): lax.ppermute(lax.slice_in_dim(block, block.shape[dim] - width, None, axis...  23.8 us
    all_gather x1, blocking collectives, on_device(): lax.all_gather(sampled.reshape(1, 1, 1, -1), 'span', axis=1, tiled=True)  16.8 us
    all_to_all x1, starting transfers between devices, on_device(): lax.all_to_all(outgoing.reshape(tile_count, CAP * 5 * spec_cols), ('span'...  13.3 us
    gather x1, local copies, waits for them, and re-layouts, on_device(): sampled = pressure[deck_cells[0, 0, 0]]  11.8 us
    dot_general x16, matrix products, add_row(): jnp.dot(row_values, member, precision=lax.Precision.HIGHEST)  9.31 us
    ppermute x6, starting transfers between devices, extended(): lax.ppermute(lax.slice_in_dim(block, 0, width, axis=dim), axis, backward)  9.23 us
  transfers between devices with their start and end apart: 13, of which 7 were waited for; matrix products, arithmetic and copies ran while one was open for 8% of the time, Pallas kernels for 0%

commit v1 on v0

--- a/solution.py
+++ b/solution.py
@@ -162,7 +162,12 @@
     traction = rows_all[0, :, 0][:, None, :] * deck_geom[0, :, 0]
     forces = strip_forces(traction, strip_ids[0, :, 0], strip_count)
     modal_part = jnp.einsum("cj,cjm->m", forces, mode_shapes, precision=lax.Precision.HIGHEST)
-    modal_force = lax.psum(modal_part, ("stream", "vert"))
+
+    def _rest_keys(z, along_axis, group_axis):
+        item_now = lax.psum(z, along_axis)
+        return lax.psum(item_now, group_axis)
+
+    modal_force = _rest_keys(modal_part, "stream", "vert")
     return (new_fields, modal_force)
 
 

time: 264 us -> 217 us (0.82)
  the two profiles are of different devices: /device:TPU:64 before, /device:TPU:24 now
where the time goes in v1:
time: 217 us
  blocking collectives  82.1 us (38%)
  starting transfers between devices  49.6 us (23%)
  other arithmetic  36.1 us (17%)
  local copies, waits for them, and re-layouts  30.7 us (14%)
  matrix products  11.3 us (5%)
  waiting for transfers between devices  4.84 us (2%)
    psum x1, blocking collectives, on_device(): lax.psum(partial_value, 'stream').reshape(5, depth_cells, span_cells)  28.1 us
    all_gather x1, blocking collectives, on_device(): lax.all_gather(sampled.reshape(1, 1, 1, -1), 'span', axis=1, tiled=True)  25.6 us
    ppermute x6, starting transfers between devices, extended(): lax.ppermute(lax.slice_in_dim(block, block.shape[dim] - width, None, axis...  24.2 us
    psum x1, blocking collectives, _rest_keys(): item_now = lax.psum(z, along_axis)  15.7 us
    all_to_all x1, starting transfers between devices, on_device(): lax.all_to_all(outgoing.reshape(tile_count, CAP * 5 * spec_cols), ('span'...  14.1 us
    psum x1, blocking collectives, _rest_keys(): return lax.psum(item_now, group_axis)  12.8 us
    gather x1, local copies, waits for them, and re-layouts, on_device(): sampled = pressure[deck_cells[0, 0, 0]]  11.8 us
    ppermute x6, starting transfers between devices, extended(): lax.ppermute(lax.slice_in_dim(block, 0, width, axis=dim), axis, backward)  11.3 us
  transfers between devices with their start and end apart: 13, of which 5 were waited for; matrix products, arithmetic and copies ran while one was open for 10% of the time, Pallas kernels for 0%

profile of v1, /device:TPU:24, one launch (start us, length us, event | category | flops | bytes accessed | tf_op | source)
XLA Modules:
  0.0 216.7 jit_solution(1224090058101289588)
XLA Ops:
  0.6 2.2 fusion.52
  3.4 2.4 %collective-permute-start = (f32[5,32,16,1]{1,2,3,0:T(8,128)S(1)}, f32[5,32,16,1]{1,2,3,0:T(8,128)S(1)}, u32[]{:S(2)}, u32[]{:S(2)}) collective-permute-start(f32[5,32,16,1]{1,2,3,0:T(8,128)S(1)} %copy.55), channel_id=1, source_target_pairs={{64,0},{128,64},{192,128},{256,192},{320,256},{384,320},{448,384},... | collective-permute-start | bytes 30728 | tf_op jit(solution)/shard_map/ppermute | solution.py:27
  6.4 4.7 %collective-permute-start.1 = (f32[5,32,16,1]{1,2,3,0:T(8,128)S(1)}, f32[5,32,16,1]{1,2,3,0:T(8,128)S(1)}, u32[]{:S(2)}, u32[]{:S(2)}) collective-permute-start(f32[5,32,16,1]{1,2,3,0:T(8,128)S(1)} %copy.56), channel_id=1, source_target_pairs={{0,64},{64,128},{128,192},{192,256},{256,320},{320,384},{384,448},... | collective-permute-start | bytes 30728 | tf_op jit(solution)/shard_map/ppermute | solution.py:24
  13.5 14.1 %all-to-all-start = ((f32[64,1,2560]{2,1,0:T(1,128)}), f32[64,1,2560]{2,1,0:T(1,128)}, u32[]{:S(2)}, u32[]{:S(2)}) async-start(f32[64,1,2560]{2,1,0:T(1,128)} %all_to_all.8), calls=%async_computation | async-start | bytes 1310720 | tf_op jit(solution)/shard_map/all_to_all | solution.py:128
  32.8 2.5 %pad_maximum_fusion.39 = (f32[5,32,1,130]{3,2,1,0:T(1,128)S(1)}, f32[5,32,1,130]{3,2,1,0:T(1,128)S(1)}) fusion(f32[5,32,16,1]{3,2,1,0:T(8,128)S(1)} %copy.37, f32[5,32,16,128]{3,2,1,0:T(8,128)S(1)} %copy-done.1, f32[5,32,16,1]{3,2,1,0:T(8,128)} %copy.39), kind=kLoop, calls=%fused_computation.121 | loop fusion | flops 83200 | bytes 1497600 | tf_op jit(solution)/shard_map/concatenate | solution.py:28
  36.6 3.0 %collective-permute-start.3 = (f32[5,32,1,130]{3,2,1,0:T(1,128)S(1)}, f32[5,32,1,130]{3,2,1,0:T(1,128)S(1)}, u32[]{:S(2)}, u32[]{:S(2)}) collective-permute-start(f32[5,32,1,130]{3,2,1,0:T(1,128)S(1)} %get-tuple-element.79), channel_id=1, source_target_pairs={{0,4},{4,8},{8,12},{12,16},{16,20},{20,24},{24,28},{28,32},{32,36}... | collective-permute-start | bytes 249608 | tf_op jit(solution)/shard_map/ppermute | solution.py:24
  42.1 4.7 %collective-permute-start.5 = (f32[5,1,18,130]{3,2,1,0:T(8,128)S(1)}, f32[5,1,18,130]{3,2,1,0:T(8,128)S(1)}, u32[]{:S(2)}, u32[]{:S(2)}) collective-permute-start(f32[5,1,18,130]{3,2,1,0:T(8,128)S(1)} %get-tuple-element.71), channel_id=1, source_target_pairs={{0,1},{1,2},{2,3},{4,5},{5,6},{6,7},{8,9},{9,10},{10,11},{12,13},{... | collective-permute-start | bytes 140408 | tf_op jit(solution)/shard_map/ppermute | solution.py:24
  49.1 3.2 %broadcast_multiply_fusion.3 = (f32[5,32,16,128]{3,2,1,0:T(8,128)S(1)}, f32[5,32,16,128]{3,2,1,0:T(8,128)S(1)}) fusion(f32[5,1,18,130]{3,2,1,0:T(8,128)S(1)} %collective-permute-done.4, f32[5,32,1,130]{3,2,1,0:T(1,128)S(1)} %collective-permute-done.2, f32[5,32,16,1]{3,2,1,0:T(8,128)S(1)} %copy.37, f32[5,32,16,128]{3,2,1,0:T(8,128)S(1)} %copy-done.1, ...), kind=kLoop, calls=%fused_computation.50 | loop fusion | flops 5242880 | bytes 4212640 | tf_op jit(solution)/shard_map/mul | solution.py:59
  56.1 2.6 %reduce = f32[64,2560]{1,0:T(8,128)S(1)} reduce(f32[64,1,2560]{2,1,0:T(1,128)} %all-to-all-done, f32[]{:T(128)} %constant.123), dimensions={1}, to_apply=%all_to_all.7.reduce_sub_computation | reduce | bytes 1310724 | tf_op jit(solution)/shard_map/all_to_all | solution.py:128
  60.5 28.1 %psum.21 = f32[5,32,16]{2,1,0:T(8,128)S(1)} all-reduce(f32[5,32,16]{2,1,0:T(8,128)S(1)} %reshape.200), channel_id=1, replica_groups=mesh['stream'=8,'span'=16,'vert'=4] {'stream'}, use_global_device_ids=true, to_apply=%region_3.4 | all-reduce | flops 2560 | bytes 20480 | tf_op jit(solution)/shard_map/psum | solution.py:144
  88.6 7.5 %multiply_add_fusion = f32[5,32,16,128]{3,2,1,0:T(8,128)S(1)} fusion(f32[5,32,16,128]{3,2,1,0:T(8,128)S(1)} %copy-done.1, f32[5,32,16,128]{3,2,1,0:T(8,128)} %broadcast_dynamic-update-slice_fusion.1, f32[5,32,16]{2,1,0:T(8,128)S(1)} %broadcast_add_fusion.1, f32[128]{0:T(128)S(1)} %compare_select_fusion.1, f32[32,16,128]{2,1,0:T(8,128)} %get-tuple-element.87, ...), kind=kLoop, calls=%fused_computation.45 | loop fusion | flops 13434880 | bytes 5009844 | tf_op jit(solution)/shard_map/add | solution.py:155
  96.1 1.9 fusion.51
  100.0 3.6 %collective-permute-start.6 = (f32[5,32,16,1]{1,2,3,0:T(8,128)S(1)}, f32[5,32,16,1]{1,2,3,0:T(8,128)S(1)}, u32[]{:S(2)}, u32[]{:S(2)}) collective-permute-start(f32[5,32,16,1]{1,2,3,0:T(8,128)S(1)} %copy.44), channel_id=1, source_target_pairs={{64,0},{128,64},{192,128},{256,192},{320,256},{384,320},{448,384},... | collective-permute-start | bytes 30728 | tf_op jit(solution)/shard_map/ppermute | solution.py:27
  105.5 3.4 %collective-permute-start.7 = (f32[5,32,16,1]{1,2,3,0:T(8,128)S(1)}, f32[5,32,16,1]{1,2,3,0:T(8,128)S(1)}, u32[]{:S(2)}, u32[]{:S(2)}) collective-permute-start(f32[5,32,16,1]{1,2,3,0:T(8,128)S(1)} %copy.46), channel_id=1, source_target_pairs={{0,64},{64,128},{128,192},{192,256},{256,320},{320,384},{384,448},... | collective-permute-start | bytes 30728 | tf_op jit(solution)/shard_map/ppermute | solution.py:24
  113.0 2.9 %pad_maximum_fusion.36 = (f32[5,32,1,130]{3,2,1,0:T(1,128)S(1)}, f32[5,32,1,130]{3,2,1,0:T(1,128)S(1)}) fusion(f32[5,32,16,1]{3,2,1,0:T(8,128)} %copy.45, f32[5,32,16,128]{3,2,1,0:T(8,128)S(1)} %multiply_add_fusion, f32[5,32,16,1]{3,2,1,0:T(8,128)} %copy.47), kind=kLoop, calls=%fused_computation.118 | loop fusion | flops 83200 | bytes 1497600 | tf_op jit(solution)/shard_map/concatenate | solution.py:28
  117.3 3.3 %collective-permute-start.9 = (f32[5,32,1,130]{3,2,1,0:T(1,128)S(1)}, f32[5,32,1,130]{3,2,1,0:T(1,128)S(1)}, u32[]{:S(2)}, u32[]{:S(2)}) collective-permute-start(f32[5,32,1,130]{3,2,1,0:T(1,128)S(1)} %get-tuple-element.75), channel_id=1, source_target_pairs={{0,4},{4,8},{8,12},{12,16},{16,20},{20,24},{24,28},{28,32},{32,36}... | collective-permute-start | bytes 249608 | tf_op jit(solution)/shard_map/ppermute | solution.py:24
  122.8 5.1 %collective-permute-start.11 = (f32[5,1,18,130]{3,2,1,0:T(8,128)S(1)}, f32[5,1,18,130]{3,2,1,0:T(8,128)S(1)}, u32[]{:S(2)}, u32[]{:S(2)}) collective-permute-start(f32[5,1,18,130]{3,2,1,0:T(8,128)S(1)} %get-tuple-element.69), channel_id=1, source_target_pairs={{0,1},{1,2},{2,3},{4,5},{5,6},{6,7},{8,9},{9,10},{10,11},{12,13},{... | collective-permute-start | bytes 140408 | tf_op jit(solution)/shard_map/ppermute | solution.py:24
  130.3 3.1 %broadcast_multiply_fusion = (f32[5,32,16,128]{3,2,1,0:T(8,128)S(1)}, f32[5,32,16,128]{3,2,1,0:T(8,128)S(1)}) fusion(f32[5,1,18,130]{3,2,1,0:T(8,128)S(1)} %collective-permute-done.10, f32[5,32,1,130]{3,2,1,0:T(1,128)S(1)} %collective-permute-done.8, f32[5,32,16,1]{3,2,1,0:T(8,128)S(1)} %copy-done.4, f32[5,32,16,128]{3,2,1,0:T(8,128)S(1)} %multiply_add_fusion, ...), kind=kLoop, calls=%fused_computation.47 | loop fusion | flops 5242880 | bytes 4212640 | tf_op jit(solution)/shard_map/mul | solution.py:59
  133.8 5.0 %add_multiply_fusion = f32[5,32,16,128]{3,2,1,0:T(8,128)S(1)} fusion(f32[5,32,16,128]{3,2,1,0:T(8,128)S(1)} %broadcast_dynamic-update-slice_fusion, f32[5,32,16,128]{3,2,1,0:T(8,128)S(1)} %multiply_add_fusion, f32[5,32,16,128]{3,2,1,0:T(8,128)S(1)} %copy-done.1, f32[32,16,128]{2,1,0:T(8,128)S(1)} %get-tuple-element.82, ...), kind=kLoop, calls=%fused_computation.44 | loop fusion | flops 14090240 | bytes 6320564 | tf_op jit(solution)/shard_map/mul | solution.py:157
  139.9 11.8 %gather_fusion = f32[2048]{0:T(1024)S(1)} fusion(f32[65536]{0:T(1024)S(1)} %bitcast.150, s32[2048]{0:T(1024)S(1)} %broadcast_clamp_fusion), kind=kCustom, calls=%fused_computation | custom fusion | bytes 24576 | tf_op jit(solution)/shard_map/gather | solution.py:159
  151.7 25.6 %all-gather = f32[32768]{0:T(1024)S(1)} all-gather(f32[2048]{0:T(1024)S(1)} %gather_fusion), channel_id=2, replica_groups=mesh['stream'=8,'span'=16,'vert'=4] {'span'}, dimensions={0}, use_global_device_ids=true | all-gather | bytes 139264 | tf_op jit(solution)/shard_map/all_gather | solution.py:161
  177.4 10.6 %while.11 = (s32[]{:T(128)}, f32[3,64]{1,0:T(4,128)S(1)}, f32[16,3,2048]{2,0,1:T(8,128)S(1)}, s32[16,2048]{1,0:T(8,128)S(1)}, s32[]{:T(128)}, /*index=5*/s32[]{:T(128)}) while((s32[]{:T(128)}, f32[3,64]{1,0:T(4,128)S(1)}, f32[16,3,2048]{2,0,1:T(8,128)S(1)}, s32[16,2048]{1,0:T(8,128)S(1)}, s32[]{:T(128)}, /*index=5*/s32[]{:T(128)}) %tuple.46), condition=%wide.region_5.6_spmd.clone, body=%wide.region_4.5_spmd.clone.sunk | while | flops 4850051 | bytes 99927 | solution.py:104
  188.2 15.7 %psum.22 = f32[32]{0:T(128)S(1)} all-reduce(f32[32]{0:T(128)S(1)} %convolution_bitcast_fusion), channel_id=1, replica_groups=mesh['stream'=8,'span'=16,'vert'=4] {'stream'}, use_global_device_ids=true, to_apply=%region_6.7 | all-reduce | flops 32 | bytes 256 | tf_op jit(solution)/shard_map/psum | solution.py:167
  203.9 12.8 %psum.23 = f32[32]{0:T(128)} all-reduce(f32[32]{0:T(128)S(1)} %psum.22), channel_id=1, replica_groups=mesh['stream'=8,'span'=16,'vert'=4] {'vert'}, use_global_device_ids=true, to_apply=%region_7.8 | all-reduce | flops 32 | bytes 256 | tf_op jit(solution)/shard_map/psum | solution.py:168
  (153 shorter events, 45.7 us)
Async XLA Ops:
  0.6 187.4 %copy-start = (f32[3,64,32]{1,2,0:T(8,128)S(1)}, f32[3,64,32]{1,2,0:T(8,128)}, u32[]{:S(2)}) copy-start(f32[3,64,32]{1,2,0:T(8,128)} %param.20) | copy-start | bytes 73732
  2.8 8.3 %copy-start.14 = (s32[64,1]{0,1:T(1,128)S(1)}, s32[64,1]{0,1:T(1,128)}, u32[]{:S(2)}) copy-start(s32[64,1]{0,1:T(1,128)} %param.16) | copy-start | bytes 772
  2.8 8.7 %copy-start.11 = (f32[64,5,256]{2,0,1:T(8,128)S(1)}, f32[64,5,256]{2,0,1:T(8,128)}, u32[]{:S(2)}) copy-start(f32[64,5,256]{2,0,1:T(8,128)} %param.15) | copy-start | bytes 983044
  3.4 27.1 %collective-permute-start = (f32[5,32,16,1]{1,2,3,0:T(8,128)S(1)}, f32[5,32,16,1]{1,2,3,0:T(8,128)S(1)}, u32[]{:S(2)}, u32[]{:S(2)}) collective-permute-start(f32[5,32,16,1]{1,2,3,0:T(8,128)S(1)} %copy.55), channel_id=1, source_target_pairs={{64,0},{128,64},{192,128},{256,192},{320,256},{384,320},{448,384},... | collective-permute-start | bytes 30728 | tf_op jit(solution)/shard_map/ppermute | solution.py:27
  6.4 24.8 %collective-permute-start.1 = (f32[5,32,16,1]{1,2,3,0:T(8,128)S(1)}, f32[5,32,16,1]{1,2,3,0:T(8,128)S(1)}, u32[]{:S(2)}, u32[]{:S(2)}) collective-permute-start(f32[5,32,16,1]{1,2,3,0:T(8,128)S(1)} %copy.56), channel_id=1, source_target_pairs={{0,64},{64,128},{128,192},{192,256},{256,320},{320,384},{384,448},... | collective-permute-start | bytes 30728 | tf_op jit(solution)/shard_map/ppermute | solution.py:24
  11.9 15.7 %copy-start.1 = (f32[5,32,16,128]{3,2,1,0:T(8,128)S(1)}, f32[5,32,16,128]{3,2,1,0:T(8,128)}, u32[]{:S(2)}) copy-start(f32[5,32,16,128]{3,2,1,0:T(8,128)} %param.13) | copy-start | bytes 3932164
  13.5 15.1 %copy-start.13 = (s32[1,1,1,2048]{3,2,1,0:T(1,128)S(1)}, s32[1,1,1,2048]{3,2,1,0:T(1,128)}, u32[]{:S(2)}) copy-start(s32[1,1,1,2048]{3,2,1,0:T(1,128)} %param.17) | copy-start | bytes 24580
  13.5 42.6 %all-to-all-start = ((f32[64,1,2560]{2,1,0:T(1,128)}), f32[64,1,2560]{2,1,0:T(1,128)}, u32[]{:S(2)}, u32[]{:S(2)}) async-start(f32[64,1,2560]{2,1,0:T(1,128)} %all_to_all.8), calls=%async_computation | async-start | bytes 1310720 | tf_op jit(solution)/shard_map/all_to_all | solution.py:128
  31.2 17.9 %copy-start.2 = (f32[5,32,16,1]{3,2,1,0:T(8,128)}, f32[5,32,16,1]{3,2,1,0:T(8,128)S(1)}, u32[]{:S(2)}) copy-start(f32[5,32,16,1]{3,2,1,0:T(8,128)S(1)} %copy.37) | copy-start | bytes 30724
  35.3 4.4 %collective-permute-start.2 = (f32[5,32,1,130]{3,2,1,0:T(1,128)S(1)}, f32[5,32,1,130]{3,2,1,0:T(1,128)S(1)}, u32[]{:S(2)}, u32[]{:S(2)}) collective-permute-start(f32[5,32,1,130]{3,2,1,0:T(1,128)S(1)} %get-tuple-element.80), channel_id=1, source_target_pairs={{4,0},{8,4},{12,8},{16,12},{20,16},{24,20},{28,24},{32,28},{36,32}... | collective-permute-start | bytes 249608 | tf_op jit(solution)/shard_map/ppermute | solution.py:27
  36.6 4.0 %collective-permute-start.3 = (f32[5,32,1,130]{3,2,1,0:T(1,128)S(1)}, f32[5,32,1,130]{3,2,1,0:T(1,128)S(1)}, u32[]{:S(2)}, u32[]{:S(2)}) collective-permute-start(f32[5,32,1,130]{3,2,1,0:T(1,128)S(1)} %get-tuple-element.79), channel_id=1, source_target_pairs={{0,4},{4,8},{8,12},{12,16},{16,20},{20,24},{24,28},{28,32},{32,36}... | collective-permute-start | bytes 249608 | tf_op jit(solution)/shard_map/ppermute | solution.py:24
  40.8 7.2 %collective-permute-start.4 = (f32[5,1,18,130]{3,2,1,0:T(8,128)S(1)}, f32[5,1,18,130]{3,2,1,0:T(8,128)S(1)}, u32[]{:S(2)}, u32[]{:S(2)}) collective-permute-start(f32[5,1,18,130]{3,2,1,0:T(8,128)S(1)} %get-tuple-element.72), channel_id=1, source_target_pairs={{1,0},{2,1},{3,2},{5,4},{6,5},{7,6},{9,8},{10,9},{11,10},{13,12},{... | collective-permute-start | bytes 140408 | tf_op jit(solution)/shard_map/ppermute | solution.py:27
  42.1 7.0 %collective-permute-start.5 = (f32[5,1,18,130]{3,2,1,0:T(8,128)S(1)}, f32[5,1,18,130]{3,2,1,0:T(8,128)S(1)}, u32[]{:S(2)}, u32[]{:S(2)}) collective-permute-start(f32[5,1,18,130]{3,2,1,0:T(8,128)S(1)} %get-tuple-element.71), channel_id=1, source_target_pairs={{0,1},{1,2},{2,3},{4,5},{5,6},{6,7},{8,9},{9,10},{10,11},{12,13},{... | collective-permute-start | bytes 140408 | tf_op jit(solution)/shard_map/ppermute | solution.py:24
  58.7 29.8 %copy-start.16 = (f32[5]{0:T(128)S(1)}, f32[5]{0:T(128)}, u32[]{:S(2)}) copy-start(f32[5]{0:T(128)} %constant.116.clone) | copy-start | bytes 64
  58.7 29.9 %copy-start.15 = (f32[5]{0:T(128)S(1)}, f32[5]{0:T(128)}, u32[]{:S(2)}) copy-start(f32[5]{0:T(128)} %constant.117.clone) | copy-start | bytes 64
  98.1 10.9 %copy-start.12 = (s32[1,16,1,2048]{3,2,1,0:T(1,128)S(1)}, s32[1,16,1,2048]{3,2,1,0:T(1,128)}, u32[]{:S(2)}) copy-start(s32[1,16,1,2048]{3,2,1,0:T(1,128)} %param.19) | copy-start | bytes 393220
  100.0 9.0 %collective-permute-start.6 = (f32[5,32,16,1]{1,2,3,0:T(8,128)S(1)}, f32[5,32,16,1]{1,2,3,0:T(8,128)S(1)}, u32[]{:S(2)}, u32[]{:S(2)}) collective-permute-start(f32[5,32,16,1]{1,2,3,0:T(8,128)S(1)} %copy.44), channel_id=1, source_target_pairs={{64,0},{128,64},{192,128},{256,192},{320,256},{384,320},{448,384},... | collective-permute-start | bytes 30728 | tf_op jit(solution)/shard_map/ppermute | solution.py:27
  105.5 5.9 %collective-permute-start.7 = (f32[5,32,16,1]{1,2,3,0:T(8,128)S(1)}, f32[5,32,16,1]{1,2,3,0:T(8,128)S(1)}, u32[]{:S(2)}, u32[]{:S(2)}) collective-permute-start(f32[5,32,16,1]{1,2,3,0:T(8,128)S(1)} %copy.46), channel_id=1, source_target_pairs={{0,64},{64,128},{128,192},{192,256},{256,320},{320,384},{384,448},... | collective-permute-start | bytes 30728 | tf_op jit(solution)/shard_map/ppermute | solution.py:24
  113.0 8.4 %copy-start.5 = (f32[5,32,16,1]{3,2,1,0:T(8,128)S(1)}, f32[5,32,16,1]{3,2,1,0:T(8,128)}, u32[]{:S(2)}) copy-start(f32[5,32,16,1]{3,2,1,0:T(8,128)} %copy.47) | copy-start | bytes 30724
  115.9 4.8 %collective-permute-start.8 = (f32[5,32,1,130]{3,2,1,0:T(1,128)S(1)}, f32[5,32,1,130]{3,2,1,0:T(1,128)S(1)}, u32[]{:S(2)}, u32[]{:S(2)}) collective-permute-start(f32[5,32,1,130]{3,2,1,0:T(1,128)S(1)} %get-tuple-element.76), channel_id=1, source_target_pairs={{4,0},{8,4},{12,8},{16,12},{20,16},{24,20},{28,24},{32,28},{36,32}... | collective-permute-start | bytes 249608 | tf_op jit(solution)/shard_map/ppermute | solution.py:27
  117.3 4.0 %collective-permute-start.9 = (f32[5,32,1,130]{3,2,1,0:T(1,128)S(1)}, f32[5,32,1,130]{3,2,1,0:T(1,128)S(1)}, u32[]{:S(2)}, u32[]{:S(2)}) collective-permute-start(f32[5,32,1,130]{3,2,1,0:T(1,128)S(1)} %get-tuple-element.75), channel_id=1, source_target_pairs={{0,4},{4,8},{8,12},{12,16},{16,20},{20,24},{24,28},{28,32},{32,36}... | collective-permute-start | bytes 249608 | tf_op jit(solution)/shard_map/ppermute | solution.py:24
  121.5 7.5 %collective-permute-start.10 = (f32[5,1,18,130]{3,2,1,0:T(8,128)S(1)}, f32[5,1,18,130]{3,2,1,0:T(8,128)S(1)}, u32[]{:S(2)}, u32[]{:S(2)}) collective-permute-start(f32[5,1,18,130]{3,2,1,0:T(8,128)S(1)} %get-tuple-element.70), channel_id=1, source_target_pairs={{1,0},{2,1},{3,2},{5,4},{6,5},{7,6},{9,8},{10,9},{11,10},{13,12},{... | collective-permute-start | bytes 140408 | tf_op jit(solution)/shard_map/ppermute | solution.py:27
  122.8 7.5 %collective-permute-start.11 = (f32[5,1,18,130]{3,2,1,0:T(8,128)S(1)}, f32[5,1,18,130]{3,2,1,0:T(8,128)S(1)}, u32[]{:S(2)}, u32[]{:S(2)}) collective-permute-start(f32[5,1,18,130]{3,2,1,0:T(8,128)S(1)} %get-tuple-element.69), channel_id=1, source_target_pairs={{0,1},{1,2},{2,3},{4,5},{5,6},{6,7},{8,9},{9,10},{10,11},{12,13},{... | collective-permute-start | bytes 140408 | tf_op jit(solution)/shard_map/ppermute | solution.py:24
  139.9 37.4 %copy-start.10 = (f32[1,16,1,3,2048]{4,2,3,1,0:T(1,128)S(1)}, f32[1,16,1,3,2048]{4,2,3,1,0:T(1,128)}, u32[]{:S(2)}) copy-start(f32[1,16,1,3,2048]{4,2,3,1,0:T(1,128)} %param.18) | copy-start | bytes 1179652
  (6 other events, 26.2 us)
